TPU v7x, 32 devices: a whole 2x2x4 slice. The times are simulated.
32 devices in a mesh: grp: 2 (over x), seq: 8 (over z, y), head: 2 (over core).
Axes of the slice: x: 2, y: 2, z: 4, core: 2. Of those that a mesh axis runs over, the one named last changes fastest.
Arguments:
- q_nope: bfloat16 [8, 128, 128], P('grp', ('seq', 'head')), parts along dimension 0, may hold values from -6 to 6
- q_rope: bfloat16 [8, 128, 64], P('grp', ('seq', 'head')), parts along dimension 0, may hold values from -150 to 150
- w_uk: bfloat16 [128, 128, 512], P(('seq', 'head')), may hold values from -0.5 to 0.5
- w_uv: bfloat16 [128, 512, 128], P(('seq', 'head')), may hold values from -1 to 1
- cache: bfloat16 [8, 4096, 576], P('grp', 'seq'), parts along dimension 0, may hold values from -12 to 12
- lengths: int32 [8], P('grp'), parts along dimension 0, may hold values from 2048 to 4096, as said below
- selected: int32 [8, 8, 32], P('grp'), parts along dimension 0, may hold values from 0 to 63, as said below
Outputs:
- attended: bfloat16 [8, 128, 128], P('grp', ('seq', 'head')), parts along dimension 0
- bounds: float32 [8, 8, 64], P('grp', None, 'seq'), parts along dimension 0
There are 2 independent parts, one for each index of `grp`. A program takes and returns all parts, laid end to end along the dimension named above; an argument that names none is the same for every part. Nothing has to cross between parts.
Inputs may be any that keep to these rules, and one draw needn't show every extreme that they name: `lengths`: some request has exactly 4096 cached tokens; every request has 2048 or more. `selected`: for each request and head group the 32 page numbers are distinct and below ceil(lengths[r] / 64); page 0 and the page of the request's last cached token are always among them.
All inputs are finite; a program needn't handle non-finite values.
Results may differ from a plain program's by a relative error of at most 0.0065.
Values may be sent and summed in bfloat16 or wider, within the bound.
A program may use at most 64 MiB of HBM per device.

v0:
```python
import jax
import jax.numpy as jnp
from jax import lax
from jax.sharding import PartitionSpec as P

GH = 16
PAGE = 64


def local(q_nope, q_rope, w_uk, w_uv, cache, lengths, selected):
    seq_count = lax.axis_size("seq")
    head_count = lax.axis_size("head")
    seq_rank = lax.axis_index("seq")
    head_rank = lax.axis_index("head")
    requests = q_nope.shape[0]
    head_block = q_nope.shape[1]
    latent_width = w_uk.shape[2]
    cache_width = cache.shape[2]
    tokens_here = cache.shape[1]
    pages_here = tokens_here // PAGE
    groups = selected.shape[1]
    softmax_scale = (q_nope.shape[2] + q_rope.shape[2]) ** (-0.5)
    query_latent = jnp.einsum(
        "rhn,hnl->rhl", q_nope, w_uk, preferred_element_type=jnp.float32
    ).astype(jnp.bfloat16)
    absorbed = jnp.concatenate([query_latent, q_rope], axis=2)
    queries = lax.all_gather(absorbed, "seq", axis=1, tiled=True)
    heads_here = head_block * seq_count
    position = jnp.arange(heads_here, dtype=jnp.int32)
    global_head = (
        position // head_block * head_count + head_rank
    ) * head_block + position % head_block
    group_of = global_head // GH
    group_hot = group_of[:, None] == jnp.arange(groups, dtype=jnp.int32)[None, :]
    page_number = seq_rank * pages_here + jnp.arange(pages_here, dtype=jnp.int32)
    token_index = seq_rank * tokens_here + jnp.arange(tokens_here, dtype=jnp.int32).reshape(
        pages_here, PAGE
    )
    live_token = token_index[None] < lengths[:, None, None]
    live_page = live_token[:, :, 0]
    page_blocks = cache.reshape(requests, pages_here, PAGE, cache_width)
    page_low = jnp.min(jnp.where(live_token[..., None], page_blocks, jnp.inf), axis=2).astype(
        jnp.float32
    )
    page_high = jnp.max(jnp.where(live_token[..., None], page_blocks, -jnp.inf), axis=2).astype(
        jnp.float32
    )
    page_low = jnp.where(live_page[..., None], page_low, 0.0)
    page_high = jnp.where(live_page[..., None], page_high, 0.0)
    middle = (page_low + page_high) * 0.5
    spread = (page_high - page_low) * 0.5
    query_float = queries.astype(jnp.float32)
    head_bound = softmax_scale * (
        jnp.einsum("rhd,rpd->rhp", query_float, middle, precision=lax.Precision.HIGHEST)
        + jnp.einsum("rhd,rpd->rhp", jnp.abs(query_float), spread, precision=lax.Precision.HIGHEST)
    )
    group_bound = jnp.max(
        jnp.where(group_hot.T[None, :, :, None], head_bound[:, None, :, :], -1e30), axis=2
    )
    group_bound = lax.pmax(group_bound, "head")
    bounds = jnp.where(live_page[:, None, :], group_bound, 0.0)
    picked = jnp.any(selected[:, :, :, None] == page_number[None, None, None, :], axis=2)
    head_pick = jnp.any(group_hot[None, :, :, None] & picked[:, None, :, :], axis=2)
    scores = (
        jnp.einsum("rhd,rtd->rht", queries, cache, preferred_element_type=jnp.float32)
        * softmax_scale
    )
    scores = scores.reshape(requests, heads_here, pages_here, PAGE)
    scores = jnp.where(live_token[:, None], scores, -1e30)
    page_top = jnp.max(scores, axis=3)
    weights = jnp.where(live_token[:, None], jnp.exp(scores - page_top[..., None]), 0.0).astype(
        jnp.bfloat16
    )
    page_total = jnp.sum(weights.astype(jnp.float32), axis=3)
    page_weighted = jnp.einsum(
        "rhpt,rptl->rhpl",
        weights,
        page_blocks[..., :latent_width],
        preferred_element_type=jnp.float32,
    )
    summit = jnp.max(jnp.where(head_pick, page_top, -1e30), axis=2)
    factor = jnp.where(head_pick, jnp.exp(page_top - summit[..., None]), 0.0)
    total = jnp.sum(factor * page_total, axis=2)
    weighted = jnp.einsum("rhp,rhpl->rhl", factor, page_weighted, precision=lax.Precision.HIGHEST)
    gotten = (
        lax.all_to_all(
            summit.reshape(requests, seq_count, head_block),
            "seq",
            split_axis=1,
            concat_axis=1,
            tiled=True,
        ),
        lax.all_to_all(
            total.reshape(requests, seq_count, head_block),
            "seq",
            split_axis=1,
            concat_axis=1,
            tiled=True,
        ),
        lax.all_to_all(
            weighted.reshape(requests, seq_count, head_block, latent_width),
            "seq",
            split_axis=1,
            concat_axis=1,
            tiled=True,
        ),
    )
    highest = jnp.max(gotten[0], axis=1)
    rescale = jnp.exp(gotten[0] - highest[:, None, :])
    own_total = jnp.sum(rescale * gotten[1], axis=1)
    own_weighted = jnp.sum(rescale[..., None] * gotten[2], axis=1)
    latent_out = (own_weighted / own_total[..., None]).astype(jnp.bfloat16)
    attended = jnp.einsum(
        "rhl,hlv->rhv", latent_out, w_uv, preferred_element_type=jnp.float32
    ).astype(jnp.bfloat16)
    return (attended, bounds)


def solution(mesh):
    placed = (
        P("grp", ("seq", "head"), None),
        P("grp", ("seq", "head"), None),
        P(("seq", "head"), None, None),
        P(("seq", "head"), None, None),
        P("grp", "seq", None),
        P("grp"),
        P("grp", None, None),
    )
    return jax.shard_map(
        local,
        mesh=mesh,
        in_specs=placed,
        out_specs=(P("grp", ("seq", "head"), None), P("grp", None, "seq")),
        check_vma=False,
    )
```

profile of v0, /device:TPU:0, one launch (start us, length us, event | category | flops | bytes accessed | tf_op | source)
XLA Modules:
  0.0 88.1 jit_solution(16813406923026156517)
XLA Ops:
  0.7 0.8 copy.102
  1.5 0.4 copy-done
  1.9 0.9 %fusion.3 = bf16[4,8,512]{2,0,1:T(4,128)(2,1)S(1)} fusion(bf16[8,128,512]{2,1,0:T(8,128)(2,1)S(1)} %copy-done, bf16[4,8,128]{2,1,0:T(8,128)(2,1)} %param.7), kind=kOutput, calls=%fused_computation.8 | convolution fusion | flops 4210688 | bytes 1089536 | tf_op jit(solution)/shard_map/rhn,hnl->rhl/dot_general | solution.py:23
  2.9 32.7 %all_gather.3 = bf16[4,64,576]{2,0,1:T(4,128)(2,1)S(1)} all-gather(bf16[4,8,576]{2,0,1:T(4,128)(2,1)S(1)} %pad_maximum_fusion), channel_id=1, replica_groups=mesh['grp'=2,'seq'=8,'head'=2] {'seq'}, dimensions={1}, use_global_device_ids=true | all-gather | bytes 331776 | tf_op jit(solution)/shard_map/all_gather | solution.py:27
  35.5 2.2 %convolution_multiply_fusion = f32[4,64,512]{2,1,0:T(8,128)S(1)} fusion(bf16[4,512,576]{1,2,0:T(8,128)(2,1)} %param.11, bf16[4,64,576]{2,0,1:T(4,128)(2,1)S(1)} %all_gather.3), kind=kOutput, calls=%fused_computation.6 | convolution fusion | flops 151126016 | bytes 3178496 | tf_op jit(solution)/shard_map/rhd,rtd->rht/dot_general | solution.py:65
  38.0 0.7 compare_reduce_fusion
  39.3 0.6 copy.105
  39.9 5.6 %all-to-all-start = ((f32[4,8,8]{2,0,1:T(4,128)}), f32[4,8,8]{2,0,1:T(4,128)S(1)}, u32[]{:S(2)}, u32[]{:S(2)}) async-start(f32[4,8,8]{2,0,1:T(4,128)} %copy.105), calls=%async_computation | async-start | bytes 32768 | tf_op jit(solution)/shard_map/all_to_all | solution.py:86
  45.5 0.7 convert_reduce_fusion
  46.2 4.3 %copy.106 = bf16[4,512,576]{2,1,0:T(8,128)(2,1)} copy(bf16[4,512,576]{1,2,0:T(8,128)(2,1)} %param.11) | data formatting | bytes 4718592 | tf_op args[4]
  50.7 2.7 %select_reduce_fusion.1 = (bf16[4,8,576]{2,1,0:T(8,128)(2,1)S(1)}, bf16[4,8,576]{2,1,0:T(8,128)(2,1)S(1)}) fusion(pred[4,8,64]{2,1,0:T(8,128)(4,1)S(1)} %broadcast_compare_fusion, bf16[4,512,576]{2,1,0:T(8,128)(2,1)} %copy.106), kind=kLoop, calls=%fused_computation.3 | loop fusion | flops 4681728 | bytes 2435072 | tf_op jit(solution)/shard_map/reduce_min | solution.py:42
  53.4 1.0 %convolution_bitcast_fusion = f32[4,64,8,512]{3,1,2,0:T(8,128)S(1)} fusion(bf16[4,8,64,576]{3,2,1,0:T(8,128)(2,1)S(1)} %bitcast.20, f32[4,64,8,64]{3,2,1,0:T(8,128)S(1)} %reshape.136, f32[4,64,8]{1,2,0:T(8,128)S(1)} %fusion.6, pred[4,8,64]{2,1,0:T(8,128)(4,1)S(1)} %broadcast_compare_fusion), kind=kOutput, calls=%fused_computation.4 | convolution fusion | flops 134742016 | bytes 7360512 | tf_op jit(solution)/shard_map/rhpt,rptl->rhpl/dot_general | solution.py:75
  54.4 5.4 %fusion = f32[4,64,1,512]{3,2,1,0:T(1,128)S(1)} fusion(f32[4,64,8,1]{2,3,1,0:T(1,128)S(1)} %copy.114, f32[4,64,8,512]{3,1,2,0:T(8,128)S(1)} %convolution_bitcast_fusion), kind=kOutput, calls=%fused_computation | convolution fusion | flops 12582912 | bytes 4726784 | tf_op jit(solution)/shard_map/rhp,rhpl->rhl/dot_general | solution.py:84
  60.0 0.6 copy.108
  60.7 6.0 %all-to-all-start.2 = ((f32[4,8,8]{2,0,1:T(4,128)}), f32[4,8,8]{2,0,1:T(4,128)S(1)}, u32[]{:S(2)}, u32[]{:S(2)}) async-start(f32[4,8,8]{2,0,1:T(4,128)} %copy.108), calls=%async_computation.2 | async-start | bytes 32768 | tf_op jit(solution)/shard_map/all_to_all | solution.py:93
  66.7 0.5 fusion.10
  67.2 0.8 copy.107
  68.0 5.3 %all-to-all-done.2 = f32[4,8,8]{2,0,1:T(4,128)S(1)} async-done(((f32[4,8,8]{2,0,1:T(4,128)}), f32[4,8,8]{2,0,1:T(4,128)S(1)}, u32[]{:S(2)}, u32[]{:S(2)}) %all-to-all-start.2) | async-done | bytes 1056 | tf_op jit(solution)/shard_map/all_to_all | solution.py:93
  73.3 3.5 %all-to-all-start.1 = ((f32[4,8,8,512]{3,2,0,1:T(8,128)}), f32[4,8,8,512]{3,2,0,1:T(8,128)S(1)}, u32[]{:S(2)}, u32[]{:S(2)}) async-start(f32[4,8,8,512]{3,2,0,1:T(8,128)} %copy.107), calls=%async_computation.1 | async-start | bytes 1048576 | tf_op jit(solution)/shard_map/all_to_all | solution.py:100
  76.8 0.8 fusion.4
  77.7 3.4 %pmax.7 = f32[4,8,8]{2,1,0:T(8,128)S(1)} all-reduce(f32[4,8,8]{2,1,0:T(8,128)S(1)} %select_reduce_fusion.2), channel_id=1, replica_groups=mesh['grp'=2,'seq'=8,'head'=2] {'head'}, use_global_device_ids=true, to_apply=%region_12.13 | all-reduce | flops 256 | bytes 2048 | tf_op jit(solution)/shard_map/pmax | solution.py:60
  81.1 0.6 broadcast_select_fusion
  81.8 5.2 %all-to-all-done.1 = f32[4,8,8,512]{3,2,0,1:T(8,128)S(1)} async-done(((f32[4,8,8,512]{3,2,0,1:T(8,128)}), f32[4,8,8,512]{3,2,0,1:T(8,128)S(1)}, u32[]{:S(2)}, u32[]{:S(2)}) %all-to-all-start.1) | async-done | bytes 524320 | tf_op jit(solution)/shard_map/all_to_all | solution.py:100
  87.4 0.6 copy.113
  (33 shorter events, 1.9 us)
Async XLA Ops:
  0.6 1.2 %copy-start = (bf16[8,128,512]{2,1,0:T(8,128)(2,1)S(1)}, bf16[8,128,512]{2,1,0:T(8,128)(2,1)}, u32[]{:S(2)}) copy-start(bf16[8,128,512]{2,1,0:T(8,128)(2,1)} %param.9) | copy-start | bytes 3145732
  2.8 35.1 %copy-start.3 = (s32[4,8,32]{2,1,0:T(8,128)S(1)}, s32[4,8,32]{2,1,0:T(8,128)}, u32[]{:S(2)}) copy-start(s32[4,8,32]{2,1,0:T(8,128)} %param.13) | copy-start | bytes 12292
  2.8 36.0 %copy-start.4 = (s32[4]{0:T(128)S(1)}, s32[4]{0:T(128)}, u32[]{:S(2)}) copy-start(s32[4]{0:T(128)} %param.12) | copy-start | bytes 52
  39.9 20.7 %all-to-all-start = ((f32[4,8,8]{2,0,1:T(4,128)}), f32[4,8,8]{2,0,1:T(4,128)S(1)}, u32[]{:S(2)}, u32[]{:S(2)}) async-start(f32[4,8,8]{2,0,1:T(4,128)} %copy.105), calls=%async_computation | async-start | bytes 32768 | tf_op jit(solution)/shard_map/all_to_all | solution.py:86
  50.7 2.7 %copy-start.1 = (bf16[4,512,576]{2,1,0:T(8,128)(2,1)S(1)}, bf16[4,512,576]{2,1,0:T(8,128)(2,1)}, u32[]{:S(2)}) copy-start(bf16[4,512,576]{2,1,0:T(8,128)(2,1)} %copy.106) | copy-start | bytes 7077892
  60.7 12.6 %all-to-all-start.2 = ((f32[4,8,8]{2,0,1:T(4,128)}), f32[4,8,8]{2,0,1:T(4,128)S(1)}, u32[]{:S(2)}, u32[]{:S(2)}) async-start(f32[4,8,8]{2,0,1:T(4,128)} %copy.108), calls=%async_computation.2 | async-start | bytes 32768 | tf_op jit(solution)/shard_map/all_to_all | solution.py:93
  66.7 20.5 %copy-start.2 = (bf16[8,512,128]{2,1,0:T(8,128)(2,1)S(1)}, bf16[8,512,128]{2,1,0:T(8,128)(2,1)}, u32[]{:S(2)}) copy-start(bf16[8,512,128]{2,1,0:T(8,128)(2,1)} %param.10) | copy-start | bytes 3145732
  73.3 13.7 %all-to-all-start.1 = ((f32[4,8,8,512]{3,2,0,1:T(8,128)}), f32[4,8,8,512]{3,2,0,1:T(8,128)S(1)}, u32[]{:S(2)}, u32[]{:S(2)}) async-start(f32[4,8,8,512]{3,2,0,1:T(8,128)} %copy.107), calls=%async_computation.1 | async-start | bytes 1048576 | tf_op jit(solution)/shard_map/all_to_all | solution.py:100
where the time goes:
time: 88.6 us; the launch traced here: 88.1 us
  blocking collectives  36 us (41%)
  starting transfers between devices  15.1 us (17%)
  matrix products  11 us (12%)
  waiting for transfers between devices  10.5 us (12%)
  local copies, waits for them, and re-layouts  8.85 us (10%)
  other arithmetic  5.68 us (6%)
    all_gather x1, blocking collectives, local(): queries = lax.all_gather(absorbed, 'seq', axis=1, tiled=True)  32.7 us
    unnamed x13, local copies, waits for them, and re-layouts  6.15 us
    all_to_all x1, starting transfers between devices, local(): lax.all_to_all(total.reshape(requests, seq_count, head_block), 'seq', spl...  6.01 us
    all_to_all x1, starting transfers between devices, local(): lax.all_to_all(summit.reshape(requests, seq_count, head_block), 'seq', sp...  5.61 us
    dot_general x1, matrix products, local(): jnp.einsum('rhp,rhpl->rhl', factor, page_weighted, precision=lax.Precisio...  5.37 us
    all_to_all x1, waiting for transfers between devices, local(): lax.all_to_all(total.reshape(requests, seq_count, head_block), 'seq', spl...  5.28 us
    all_to_all x1, waiting for transfers between devices, local(): lax.all_to_all(weighted.reshape(requests, seq_count, head_block, latent_w...  5.23 us
    all_to_all x1, starting transfers between devices, local(): lax.all_to_all(weighted.reshape(requests, seq_count, head_block, latent_w...  3.49 us
  transfers between devices with their start and end apart: 3, of which 2 were waited for; matrix products, arithmetic and copies ran while one was open for 20% of the time, Pallas kernels for 0%

commit v1 on v0

v1 whole, which is shorter than its diff:
```python
import functools

import jax
import jax.numpy as jnp
from jax import lax
from jax.experimental import pallas as pl
from jax.experimental.pallas import tpu as pltpu
from jax.sharding import PartitionSpec as P

GH = 16
PAGE = 64
LOWEST = -1e30
FLOOR = -1e29
NT = (((1,), (1,)), ((), ()))


def kernel(
    n, hc, R, hb, T, DL, D, groups, scale,
    len_ref, qn_ref, qr_ref, sel_ref, wuk_hbm, wuv_hbm, cache_hbm,
    out_ref, bounds_ref,
    wuk, wuv, cache, gq, qf, pen, hi_s, lo_s, so, st, ro, rs, gb, gbr,
    in_sem, q_send, q_recv, o_send, o_recv, s_send, s_recv, b_send, b_recv,
):
    f32, bf16 = jnp.float32, jnp.bfloat16
    me = lax.axis_index("seq")
    hr = lax.axis_index("head")
    H = n * hb
    chunks = so.shape[0]
    RC = R // chunks
    pages = T // PAGE

    load_uk = pltpu.make_async_copy(wuk_hbm, wuk, in_sem.at[0])
    load_cache = [
        pltpu.make_async_copy(cache_hbm.at[r], cache.at[r], in_sem.at[2 + r]) for r in range(R)
    ]
    load_uv = pltpu.make_async_copy(wuv_hbm, wuv, in_sem.at[1])
    load_uk.start()
    for c in load_cache:
        c.start()
    load_uv.start()

    barrier = pltpu.get_barrier_semaphore()
    for k in range(1, n):
        pl.semaphore_signal(barrier, inc=1, device_id={"seq": lax.rem(me + k, n)})
    for k in range(1, hc):
        pl.semaphore_signal(barrier, inc=1, device_id={"head": lax.rem(hr + k, hc)})

    def spread(rows, width):
        which = lax.rem(lax.broadcasted_iota(jnp.int32, (R * hb, width), 0), hb)
        return jnp.concatenate(
            [jnp.where(which == h, rows, 0.0).astype(bf16) for h in range(hb)], axis=1
        )

    qn = jnp.concatenate([qn_ref[r].astype(f32) for r in range(R)], axis=0)
    qr = jnp.concatenate([qr_ref[r].astype(f32) for r in range(R)], axis=0)
    lhs = spread(qn, qn.shape[1])
    load_uk.wait()
    latent = jnp.dot(lhs, wuk[...].reshape(lhs.shape[1], DL), preferred_element_type=f32)
    gq[me, :, :DL] = latent.astype(bf16)
    gq[me, :, DL:] = qr.astype(bf16)

    pl.semaphore_wait(barrier, n - 1 + hc - 1)
    q_copies = []
    for k in range(1, n):
        c = pltpu.make_async_remote_copy(
            src_ref=gq.at[me], dst_ref=gq.at[me], send_sem=q_send.at[k], recv_sem=q_recv.at[k],
            device_id={"seq": lax.rem(me + k, n)},
        )
        c.start()
        q_copies.append(c)

    row_head = lax.broadcasted_iota(jnp.int32, (H, groups), 0)
    row_head = (lax.div(row_head, hb) * hc + hr) * hb + lax.rem(row_head, hb)
    hot = lax.div(row_head, GH) == lax.broadcasted_iota(jnp.int32, (H, groups), 1)
    hot_b = jnp.where(hot, 1.0, 0.0).astype(bf16)
    tok = me * T + lax.broadcasted_iota(jnp.int32, (groups, T), 1)
    page_of = lax.div(tok, PAGE)
    tok_col = me * T + lax.broadcasted_iota(jnp.int32, (T, 1), 0)
    page_col = (me * pages + lax.broadcasted_iota(jnp.int32, (pages, 1), 0)) * PAGE
    for r in range(R):
        length = len_ref[r]
        sel = sel_ref[r]
        hit = jnp.zeros((groups, T), f32)
        for k in range(sel.shape[1]):
            hit = jnp.where(sel[:, k:k + 1] == page_of, 1.0, hit)
        hit = jnp.where(tok < length, hit, 0.0)
        mask = jnp.dot(hot_b, hit.astype(bf16), preferred_element_type=f32)
        pen[r] = (1.0 - mask) * LOWEST
    for r in range(R):
        length = len_ref[r]
        load_cache[r].wait()
        x = cache[r].astype(f32)
        live = tok_col < length
        low = jnp.min(jnp.where(live, x, jnp.inf).reshape(pages, PAGE, D), axis=1)
        high = jnp.max(jnp.where(live, x, -jnp.inf).reshape(pages, PAGE, D), axis=1)
        live_page = page_col < length
        lo_s[r] = jnp.where(live_page, low, 0.0).astype(bf16)
        hi_s[r] = jnp.where(live_page, high, 0.0).astype(bf16)

    for c in q_copies:
        c.wait_recv()
    for s in range(n):
        block = gq[s].astype(f32)
        for r in range(R):
            qf[r, s * hb:(s + 1) * hb, :] = block[r * hb:(r + 1) * hb]

    lane = lax.broadcasted_iota(jnp.int32, (H, 128), 1)
    tops = jnp.zeros((H, 128), f32)
    sums = jnp.ones((H, 128), f32)
    o_copies = []
    for c in range(chunks):
        outs = []
        for r in range(c * RC, (c + 1) * RC):
            q = qf[r].astype(bf16)
            s = lax.dot_general(q, cache[r], NT, preferred_element_type=f32) * scale + pen[r]
            m = jnp.maximum(jnp.max(s, axis=1, keepdims=True), FLOOR)
            w = jnp.exp(s - m).astype(bf16)
            l = jnp.sum(w.astype(f32), axis=1, keepdims=True)
            outs.append(jnp.dot(w, cache[r, :, :DL], preferred_element_type=f32))
            tops = jnp.where(lane == r, m, tops)
            sums = jnp.where(lane == r, l, sums)
        for b in range(n):
            so[c, b] = jnp.concatenate(
                [o[b * hb:(b + 1) * hb] for o in outs], axis=0
            ).astype(bf16)
        if c == chunks - 1:
            for b in range(n):
                st[b, 0] = tops[b * hb:(b + 1) * hb]
                st[b, 1] = sums[b * hb:(b + 1) * hb]
        for k in range(1, n):
            to = lax.rem(me + k, n)
            cp = pltpu.make_async_remote_copy(
                src_ref=so.at[c, to], dst_ref=ro.at[c, me],
                send_sem=o_send.at[c, k], recv_sem=o_recv.at[c, k], device_id={"seq": to},
            )
            cp.start()
            o_copies.append(cp)
            if c == chunks - 1:
                cp = pltpu.make_async_remote_copy(
                    src_ref=st.at[to], dst_ref=rs.at[me],
                    send_sem=s_send.at[k], recv_sem=s_recv.at[k], device_id={"seq": to},
                )
                cp.start()
                o_copies.append(cp)

    parts = []
    for r in range(R):
        q = qf[r]
        above = jnp.maximum(q, 0.0).astype(bf16)
        below = jnp.minimum(q, 0.0).astype(bf16)
        parts.append(
            lax.dot_general(above, hi_s[r], NT, preferred_element_type=f32)
            + lax.dot_general(below, lo_s[r], NT, preferred_element_type=f32)
        )
    parts.append(jnp.zeros((H, 128 - R * pages), f32))
    head_bound = jnp.concatenate(parts, axis=1) * scale
    gb[...] = jnp.concatenate(
        [
            jnp.max(jnp.where(hot[:, g:g + 1], head_bound, LOWEST), axis=0, keepdims=True)
            for g in range(groups)
        ],
        axis=0,
    )
    b_copies = []
    for k in range(1, hc):
        cp = pltpu.make_async_remote_copy(
            src_ref=gb, dst_ref=gbr.at[k], send_sem=b_send.at[k], recv_sem=b_recv.at[k],
            device_id={"head": lax.rem(hr + k, hc)},
        )
        cp.start()
        b_copies.append(cp)
    for c in range(chunks):
        ro[c, me] = so[c, me]
    rs[me] = st[me]
    load_uv.wait()
    for cp in b_copies:
        cp.wait_recv()
    best = gb[...]
    for k in range(1, hc):
        best = jnp.maximum(best, gbr[k])
    page_row = (me * pages + lax.broadcasted_iota(jnp.int32, (groups, pages), 1)) * PAGE
    for r in range(R):
        bounds_ref[r] = jnp.where(
            page_row < len_ref[r], best[:, r * pages:(r + 1) * pages], 0.0
        )

    for cp in o_copies:
        cp.wait_recv()
    peak = rs[0, 0]
    for b in range(1, n):
        peak = jnp.maximum(peak, rs[b, 0])
    shares = [jnp.exp(rs[b, 0] - peak) for b in range(n)]
    total = shares[0] * rs[0, 1]
    for b in range(1, n):
        total += shares[b] * rs[b, 1]
    shares = [x / total for x in shares]
    rows = []
    for c in range(chunks):
        acc = [jnp.zeros((hb, DL), f32) for _ in range(RC)]
        for b in range(n):
            block = ro[c, b].astype(f32)
            for i in range(RC):
                r = c * RC + i
                acc[i] += shares[b][:, r:r + 1] * block[i * hb:(i + 1) * hb]
        rows += acc
    lhs = spread(jnp.concatenate(rows, axis=0), DL)
    res = jnp.dot(lhs, wuv[...].reshape(lhs.shape[1], wuv.shape[2]), preferred_element_type=f32)
    for r in range(R):
        out_ref[r] = res[r * hb:(r + 1) * hb].astype(bf16)
    for cp in q_copies + o_copies + b_copies:
        cp.wait_send()


def local(n, hc, q_nope, q_rope, w_uk, w_uv, cache, lengths, selected):
    R, hb, DN = q_nope.shape
    DL, DV = w_uk.shape[2], w_uv.shape[2]
    T, D = cache.shape[1:]
    groups = selected.shape[1]
    pages = T // PAGE
    H = n * hb
    chunks = 2 if R % 2 == 0 else 1
    scale = (DN + q_rope.shape[2]) ** (-0.5)
    f32, bf16 = jnp.float32, jnp.bfloat16
    V = pltpu.VMEM
    vm = pl.BlockSpec(memory_space=pltpu.VMEM)
    hbm = pl.BlockSpec(memory_space=pl.ANY)
    dma = pltpu.SemaphoreType.DMA
    return pl.pallas_call(
        functools.partial(kernel, n, hc, R, hb, T, DL, D, groups, scale),
        out_shape=(
            jax.ShapeDtypeStruct((R, hb, DV), bf16),
            jax.ShapeDtypeStruct((R, groups, pages), f32),
        ),
        in_specs=[pl.BlockSpec(memory_space=pltpu.SMEM), vm, vm, vm, hbm, hbm, hbm],
        out_specs=(vm, vm),
        scratch_shapes=[
            V((hb, DN, DL), bf16),
            V((hb, DL, DV), bf16),
            V((R, T, D), bf16),
            V((n, R * hb, D), bf16),
            V((R, H, D), f32),
            V((R, H, T), f32),
            V((R, pages, D), bf16),
            V((R, pages, D), bf16),
            V((chunks, n, R // chunks * hb, DL), bf16),
            V((n, 2, hb, 128), f32),
            V((chunks, n, R // chunks * hb, DL), bf16),
            V((n, 2, hb, 128), f32),
            V((groups, 128), f32),
            V((hc, groups, 128), f32),
            dma((2 + R,)),
            dma((n,)), dma((n,)),
            dma((chunks, n)), dma((chunks, n)),
            dma((n,)), dma((n,)),
            dma((hc,)), dma((hc,)),
        ],
        compiler_params=pltpu.CompilerParams(
            collective_id=0, has_side_effects=True, vmem_limit_bytes=40 * 1024 * 1024
        ),
    )(lengths, q_nope, q_rope, selected, w_uk, w_uv, cache)


def solution(mesh):
    placed = (
        P("grp", ("seq", "head"), None),
        P("grp", ("seq", "head"), None),
        P(("seq", "head"), None, None),
        P(("seq", "head"), None, None),
        P("grp", "seq", None),
        P("grp"),
        P("grp", None, None),
    )
    return jax.shard_map(
        functools.partial(local, mesh.shape["seq"], mesh.shape["head"]),
        mesh=mesh,
        in_specs=placed,
        out_specs=(P("grp", ("seq", "head"), None), P("grp", None, "seq")),
        check_vma=False,
    )
```

time: 88.6 us -> 31.6 us (0.36)
  blocking collectives: 36 us -> 0 us
  Pallas kernels: 0 us -> 23.9 us
  starting transfers between devices: 15.1 us -> 0 us
  matrix products: 11 us -> 0 us
  waiting for transfers between devices: 10.5 us -> 0 us
  other arithmetic: 5.68 us -> 0 us
  local copies, waits for them, and re-layouts: 8.85 us -> 6.78 us
    all_gather x1 -> x0, blocking collectives: 32.7 us -> none  [local(): queries = lax.all_gather(absorbed, 'seq', axis=1, tiled=True)]
    pallas_call x0 -> x1, Pallas kernels: none -> 23.9 us  [local(): pl.pallas_call(functools.partial(kernel, n, hc, R, hb, T, DL, D, groups,...]
    all_to_all x3 -> x0, starting transfers between devices: 15.1 us -> none  [the longest x1 6.01 us: local(): lax.all_to_all(total.reshape(requests, seq_count, head_block), 'seq', spl...]
    dot_general x7 -> x0, matrix products: 11 us -> none  [the longest x1 5.37 us: local(): jnp.einsum('rhp,rhpl->rhl', factor, page_weighted, precision=lax.Precisio...]
    all_to_all x3 -> x0, waiting for transfers between devices: 10.5 us -> none  [the longest x1 5.28 us: local(): lax.all_to_all(total.reshape(requests, seq_count, head_block), 'seq', spl...]
    pmax x1 -> x0, blocking collectives: 3.36 us -> none  [local(): group_bound = lax.pmax(group_bound, 'head')]
    reduce_min x1 -> x0, other arithmetic: 2.68 us -> none  [local(): jnp.min(jnp.where(live_token[..., None], page_blocks, jnp.inf), axis=2)]
    reshape x6 -> x0, local copies, waits for them, and re-layouts: 2.42 us -> none  [the longest x1 0.83 us: local(): weighted.reshape(requests, seq_count, head_block, latent_width)]
  transfers between devices with their start and end apart: 3 -> 0, of which waited for: 2 -> 0; matrix products, arithmetic and copies ran while one was open for 20% -> 0% of each run, Pallas kernels for 0% -> 0%
where the time goes in v1:
time: 31.6 us; the launch traced here: 31.4 us
  Pallas kernels  23.9 us (76%)
  local copies, waits for them, and re-layouts  6.78 us (21%)
  between operations  0.72 us (2%)
    pallas_call x1, Pallas kernels, local(): pl.pallas_call(functools.partial(kernel, n, hc, R, hb, T, DL, D, groups,...  23.9 us
    unnamed x15, local copies, waits for them, and re-layouts  6.78 us

profile of v1, /device:TPU:0, one launch (start us, length us, event | category | flops | bytes accessed | tf_op | source)
XLA Modules:
  0.0 31.4 jit_solution(14636827220906882569)
XLA Ops:
  0.6 0.0 copy-start.2
  0.6 0.0 copy-start.5
  0.7 0.0 copy-start.4
  0.7 0.0 copy-start.3
  0.7 3.1 %copy.9.cache_hbm = bf16[4,512,576]{2,1,0:T(8,128)(2,1)S(1)} copy(bf16[4,512,576]{1,2,0:T(8,128)(2,1)} %param.11) | data formatting | bytes 4718592 | tf_op args[4]
  3.8 0.0 copy-done.2
  3.8 0.0 copy-done.5
  3.8 0.0 copy-done.4
  3.8 0.0 copy-done.3
  3.8 0.0 copy-start
  3.8 1.2 %copy-done = bf16[8,128,512]{2,1,0:T(8,128)(2,1)S(1)} copy-done((bf16[8,128,512]{2,1,0:T(8,128)(2,1)S(1)}, bf16[8,128,512]{2,1,0:T(8,128)(2,1)}, u32[]{:S(2)}) %copy-start) | copy-done | bytes 1048600
  5.1 0.0 copy-start.1
  5.1 1.2 %copy-done.1 = bf16[8,512,128]{2,1,0:T(8,128)(2,1)S(1)} copy-done((bf16[8,512,128]{2,1,0:T(8,128)(2,1)S(1)}, bf16[8,512,128]{2,1,0:T(8,128)(2,1)}, u32[]{:S(2)}) %copy-start.1) | copy-done | bytes 1048600
  6.3 23.9 %shard_map.86 = (bf16[4,8,128]{2,1,0:T(8,128)(2,1)S(1)}, f32[4,8,8]{2,1,0:T(8,128)S(1)}) custom-call(s32[4]{0:T(128)S(1)} %copy-done.5, bf16[4,8,128]{2,1,0:T(8,128)(2,1)S(1)} %copy-done.3, bf16[4,8,64]{2,1,0:T(8,128)(2,1)S(1)} %copy-done.4, s32[4,8,32]{2,1,0:T(8,128)S(1)} %copy-done.2, bf16[8,128,512]{2,1,0:T(8,128)(2,1)S(1)} %copy-done, ...), custom_call_target="tpu_custom_call" | custom-call | tf_op jit(solution)/shard_map/pallas_call | solution.py:228
  30.2 0.6 %copy.12 = bf16[4,8,128]{2,1,0:T(8,128)(2,1)} copy(bf16[4,8,128]{2,1,0:T(8,128)(2,1)S(1)} %get-tuple-element.4) | data formatting | bytes 16384
  30.8 0.6 %copy.13 = f32[4,8,8]{2,1,0:T(8,128)} copy(f32[4,8,8]{2,1,0:T(8,128)S(1)} %get-tuple-element.5) | data formatting | bytes 2048
Async XLA Ops:
  0.6 3.2 %copy-start.2 = (s32[4,8,32]{2,1,0:T(8,128)S(1)}, s32[4,8,32]{2,1,0:T(8,128)}, u32[]{:S(2)}) copy-start(s32[4,8,32]{2,1,0:T(8,128)} %sel_ref.1) | copy-start | bytes 12292
  0.6 3.2 %copy-start.5 = (s32[4]{0:T(128)S(1)}, s32[4]{0:T(128)}, u32[]{:S(2)}) copy-start(s32[4]{0:T(128)} %len_ref.1) | copy-start | bytes 52
  0.7 3.2 %copy-start.4 = (bf16[4,8,64]{2,1,0:T(8,128)(2,1)S(1)}, bf16[4,8,64]{2,1,0:T(8,128)(2,1)}, u32[]{:S(2)}) copy-start(bf16[4,8,64]{2,1,0:T(8,128)(2,1)} %qr_ref.1) | copy-start | bytes 12292
  0.7 3.2 %copy-start.3 = (bf16[4,8,128]{2,1,0:T(8,128)(2,1)S(1)}, bf16[4,8,128]{2,1,0:T(8,128)(2,1)}, u32[]{:S(2)}) copy-start(bf16[4,8,128]{2,1,0:T(8,128)(2,1)} %qn_ref.1) | copy-start | bytes 24580
  3.8 1.2 %copy-start = (bf16[8,128,512]{2,1,0:T(8,128)(2,1)S(1)}, bf16[8,128,512]{2,1,0:T(8,128)(2,1)}, u32[]{:S(2)}) copy-start(bf16[8,128,512]{2,1,0:T(8,128)(2,1)} %wuk_hbm.1) | copy-start | bytes 3145732
  5.1 1.2 %copy-start.1 = (bf16[8,512,128]{2,1,0:T(8,128)(2,1)S(1)}, bf16[8,512,128]{2,1,0:T(8,128)(2,1)}, u32[]{:S(2)}) copy-start(bf16[8,512,128]{2,1,0:T(8,128)(2,1)} %wuv_hbm.1) | copy-start | bytes 3145732

commit v2 on v1

--- a/solution.py
+++ b/solution.py
@@ -19,7 +19,7 @@
     len_ref, qn_ref, qr_ref, sel_ref, wuk_hbm, wuv_hbm, cache_hbm,
     out_ref, bounds_ref,
     wuk, wuv, cache, gq, qf, pen, hi_s, lo_s, so, st, ro, rs, gb, gbr,
-    in_sem, q_send, q_recv, o_send, o_recv, s_send, s_recv, b_send, b_recv,
+    in_sem, uk_sem, q_send, q_recv, o_send, o_recv, s_send, s_recv, b_send, b_recv,
 ):
     f32, bf16 = jnp.float32, jnp.bfloat16
     me = lax.axis_index("seq")
@@ -29,15 +29,15 @@
     RC = R // chunks
     pages = T // PAGE
 
-    load_uk = pltpu.make_async_copy(wuk_hbm, wuk, in_sem.at[0])
+    load_uk = [
+        pltpu.make_async_copy(wuk_hbm.at[h], wuk.at[h], uk_sem.at[h]) for h in range(hb)
+    ]
     load_cache = [
         pltpu.make_async_copy(cache_hbm.at[r], cache.at[r], in_sem.at[2 + r]) for r in range(R)
     ]
     load_uv = pltpu.make_async_copy(wuv_hbm, wuv, in_sem.at[1])
-    load_uk.start()
-    for c in load_cache:
+    for c in load_uk:
         c.start()
-    load_uv.start()
 
     barrier = pltpu.get_barrier_semaphore()
     for k in range(1, n):
@@ -54,20 +54,28 @@
     qn = jnp.concatenate([qn_ref[r].astype(f32) for r in range(R)], axis=0)
     qr = jnp.concatenate([qr_ref[r].astype(f32) for r in range(R)], axis=0)
     lhs = spread(qn, qn.shape[1])
-    load_uk.wait()
+    for c in load_uk:
+        c.wait()
+    for c in load_cache:
+        c.start()
+    load_uv.start()
     latent = jnp.dot(lhs, wuk[...].reshape(lhs.shape[1], DL), preferred_element_type=f32)
-    gq[me, :, :DL] = latent.astype(bf16)
-    gq[me, :, DL:] = qr.astype(bf16)
+    RH = RC * hb
+    for c in range(chunks):
+        gq[c, me, :, :DL] = latent[c * RH:(c + 1) * RH].astype(bf16)
+        gq[c, me, :, DL:] = qr[c * RH:(c + 1) * RH].astype(bf16)
 
     pl.semaphore_wait(barrier, n - 1 + hc - 1)
-    q_copies = []
-    for k in range(1, n):
-        c = pltpu.make_async_remote_copy(
-            src_ref=gq.at[me], dst_ref=gq.at[me], send_sem=q_send.at[k], recv_sem=q_recv.at[k],
-            device_id={"seq": lax.rem(me + k, n)},
-        )
-        c.start()
-        q_copies.append(c)
+    q_copies = [[] for _ in range(chunks)]
+    for c in range(chunks):
+        for k in range(1, n):
+            cp = pltpu.make_async_remote_copy(
+                src_ref=gq.at[c, me], dst_ref=gq.at[c, me],
+                send_sem=q_send.at[c, k], recv_sem=q_recv.at[c, k],
+                device_id={"seq": lax.rem(me + k, n)},
+            )
+            cp.start()
+            q_copies[c].append(cp)
 
     row_head = lax.broadcasted_iota(jnp.int32, (H, groups), 0)
     row_head = (lax.div(row_head, hb) * hc + hr) * hb + lax.rem(row_head, hb)
@@ -86,10 +94,23 @@
         hit = jnp.where(tok < length, hit, 0.0)
         mask = jnp.dot(hot_b, hit.astype(bf16), preferred_element_type=f32)
         pen[r] = (1.0 - mask) * LOWEST
+    TILE = 128 if T % 128 == 0 else T
+    eye = jnp.where(
+        lax.broadcasted_iota(jnp.int32, (TILE, TILE), 0)
+        == lax.broadcasted_iota(jnp.int32, (TILE, TILE), 1), 1.0, 0.0
+    ).astype(bf16)
     for r in range(R):
         length = len_ref[r]
         load_cache[r].wait()
-        x = cache[r].astype(f32)
+        x = jnp.concatenate(
+            [
+                lax.dot_general(
+                    eye, cache[r, :, t * TILE:(t + 1) * TILE], NT, preferred_element_type=f32
+                )
+                for t in range(T // TILE)
+            ],
+            axis=0,
+        )
         live = tok_col < length
         low = jnp.min(jnp.where(live, x, jnp.inf).reshape(pages, PAGE, D), axis=1)
         high = jnp.max(jnp.where(live, x, -jnp.inf).reshape(pages, PAGE, D), axis=1)
@@ -97,26 +118,25 @@
         lo_s[r] = jnp.where(live_page, low, 0.0).astype(bf16)
         hi_s[r] = jnp.where(live_page, high, 0.0).astype(bf16)
 
-    for c in q_copies:
-        c.wait_recv()
-    for s in range(n):
-        block = gq[s].astype(f32)
-        for r in range(R):
-            qf[r, s * hb:(s + 1) * hb, :] = block[r * hb:(r + 1) * hb]
-
     lane = lax.broadcasted_iota(jnp.int32, (H, 128), 1)
     tops = jnp.zeros((H, 128), f32)
     sums = jnp.ones((H, 128), f32)
     o_copies = []
     for c in range(chunks):
         outs = []
+        for cp in q_copies[c]:
+            cp.wait_recv()
+        for b in range(n):
+            block = gq[c, b].astype(f32)
+            for i in range(RC):
+                qf[c * RC + i, b * hb:(b + 1) * hb, :] = block[i * hb:(i + 1) * hb]
         for r in range(c * RC, (c + 1) * RC):
             q = qf[r].astype(bf16)
-            s = lax.dot_general(q, cache[r], NT, preferred_element_type=f32) * scale + pen[r]
+            s = jnp.dot(q, cache[r], preferred_element_type=f32) * scale + pen[r]
             m = jnp.maximum(jnp.max(s, axis=1, keepdims=True), FLOOR)
             w = jnp.exp(s - m).astype(bf16)
             l = jnp.sum(w.astype(f32), axis=1, keepdims=True)
-            outs.append(jnp.dot(w, cache[r, :, :DL], preferred_element_type=f32))
+            outs.append(lax.dot_general(w, cache[r, :DL, :], NT, preferred_element_type=f32))
             tops = jnp.where(lane == r, m, tops)
             sums = jnp.where(lane == r, l, sums)
         for b in range(n):
@@ -207,7 +227,7 @@
     res = jnp.dot(lhs, wuv[...].reshape(lhs.shape[1], wuv.shape[2]), preferred_element_type=f32)
     for r in range(R):
         out_ref[r] = res[r * hb:(r + 1) * hb].astype(bf16)
-    for cp in q_copies + o_copies + b_copies:
+    for cp in sum(q_copies, []) + o_copies + b_copies:
         cp.wait_send()
 
 
@@ -236,8 +256,8 @@
         scratch_shapes=[
             V((hb, DN, DL), bf16),
             V((hb, DL, DV), bf16),
-            V((R, T, D), bf16),
-            V((n, R * hb, D), bf16),
+            V((R, D, T), bf16),
+            V((chunks, n, R // chunks * hb, D), bf16),
             V((R, H, D), f32),
             V((R, H, T), f32),
             V((R, pages, D), bf16),
@@ -249,15 +269,16 @@
             V((groups, 128), f32),
             V((hc, groups, 128), f32),
             dma((2 + R,)),
-            dma((n,)), dma((n,)),
+            dma((hb,)),
+            dma((chunks, n)), dma((chunks, n)),
             dma((chunks, n)), dma((chunks, n)),
             dma((n,)), dma((n,)),
             dma((hc,)), dma((hc,)),
         ],
         compiler_params=pltpu.CompilerParams(
-            collective_id=0, has_side_effects=True, vmem_limit_bytes=40 * 1024 * 1024
+            collective_id=0, has_side_effects=True
         ),
-    )(lengths, q_nope, q_rope, selected, w_uk, w_uv, cache)
+    )(lengths, q_nope, q_rope, selected, w_uk, w_uv, jnp.swapaxes(cache, 1, 2))
 
 
 def solution(mesh):

time: 31.6 us -> 28.4 us (0.90)
  local copies, waits for them, and re-layouts: 6.78 us -> 2.62 us
  Pallas kernels: 23.9 us -> 24.7 us
    unnamed x15 -> x2, local copies, waits for them, and re-layouts: 6.78 us -> 2.62 us
    pallas_call x1, Pallas kernels: 23.9 us -> 24.7 us  [local(): pl.pallas_call(functools.partial(kernel, n, hc, R, hb, T, DL, D, groups,...]
where the time goes in v2:
time: 28.4 us; the launch traced here: 28 us
  Pallas kernels  24.7 us (87%)
  local copies, waits for them, and re-layouts  2.62 us (9%)
  between operations  0.64 us (2%)
    pallas_call x1, Pallas kernels, local(): pl.pallas_call(functools.partial(kernel, n, hc, R, hb, T, DL, D, groups,...  24.7 us
    unnamed x2, local copies, waits for them, and re-layouts  2.62 us

profile of v2, /device:TPU:0, one launch (start us, length us, event | category | flops | bytes accessed | tf_op | source)
XLA Modules:
  0.0 28.0 jit_solution(13185599953357371895)
XLA Ops:
  0.6 24.7 %shard_map.86 = (bf16[4,8,128]{2,1,0:T(8,128)(2,1)}, f32[4,8,8]{2,1,0:T(8,128)}) custom-call(s32[4]{0:T(128)} %len_ref.1, bf16[4,8,128]{2,1,0:T(8,128)(2,1)} %qn_ref.1, bf16[4,8,64]{2,1,0:T(8,128)(2,1)} %qr_ref.1, s32[4,8,32]{2,1,0:T(8,128)} %sel_ref.1, bf16[8,128,512]{2,1,0:T(8,128)(2,1)} %wuk_hbm.1, bf16[8,512,128]{2,1,0:T(8,128)(2,1)} %wuv_hbm.1, ...), custom_call_target="tpu_custom_call" | custom-call | tf_op jit(solution)/shard_map/pallas_call | solution.py:248
  25.4 1.3 %copy.11 = bf16[4,8,128]{2,1,0:T(8,128)(2,1)} copy(bf16[4,8,128]{2,1,0:T(8,128)(2,1)} %get-tuple-element.4) | data formatting | bytes 16384
  26.7 1.3 %copy.12 = f32[4,8,8]{2,1,0:T(8,128)} copy(f32[4,8,8]{2,1,0:T(8,128)} %get-tuple-element.5) | data formatting | bytes 2048

commit v3 on v1

--- a/solution.py
+++ b/solution.py
@@ -19,7 +19,7 @@
     len_ref, qn_ref, qr_ref, sel_ref, wuk_hbm, wuv_hbm, cache_hbm,
     out_ref, bounds_ref,
     wuk, wuv, cache, gq, qf, pen, hi_s, lo_s, so, st, ro, rs, gb, gbr,
-    in_sem, q_send, q_recv, o_send, o_recv, s_send, s_recv, b_send, b_recv,
+    in_sem, uk_sem, q_send, q_recv, o_send, o_recv, s_send, s_recv, b_send, b_recv,
 ):
     f32, bf16 = jnp.float32, jnp.bfloat16
     me = lax.axis_index("seq")
@@ -29,15 +29,15 @@
     RC = R // chunks
     pages = T // PAGE
 
-    load_uk = pltpu.make_async_copy(wuk_hbm, wuk, in_sem.at[0])
+    load_uk = [
+        pltpu.make_async_copy(wuk_hbm.at[h], wuk.at[h], uk_sem.at[h]) for h in range(hb)
+    ]
     load_cache = [
         pltpu.make_async_copy(cache_hbm.at[r], cache.at[r], in_sem.at[2 + r]) for r in range(R)
     ]
     load_uv = pltpu.make_async_copy(wuv_hbm, wuv, in_sem.at[1])
-    load_uk.start()
-    for c in load_cache:
+    for c in load_uk:
         c.start()
-    load_uv.start()
 
     barrier = pltpu.get_barrier_semaphore()
     for k in range(1, n):
@@ -54,20 +54,40 @@
     qn = jnp.concatenate([qn_ref[r].astype(f32) for r in range(R)], axis=0)
     qr = jnp.concatenate([qr_ref[r].astype(f32) for r in range(R)], axis=0)
     lhs = spread(qn, qn.shape[1])
-    load_uk.wait()
+    for c in load_uk:
+        c.wait()
+    for c in load_cache:
+        c.start()
+    load_uv.start()
     latent = jnp.dot(lhs, wuk[...].reshape(lhs.shape[1], DL), preferred_element_type=f32)
-    gq[me, :, :DL] = latent.astype(bf16)
-    gq[me, :, DL:] = qr.astype(bf16)
+    RH = RC * hb
+    for c in range(chunks):
+        gq[c, me, :, :DL] = latent[c * RH:(c + 1) * RH].astype(bf16)
+        gq[c, me, :, DL:] = qr[c * RH:(c + 1) * RH].astype(bf16)
 
     pl.semaphore_wait(barrier, n - 1 + hc - 1)
-    q_copies = []
-    for k in range(1, n):
-        c = pltpu.make_async_remote_copy(
-            src_ref=gq.at[me], dst_ref=gq.at[me], send_sem=q_send.at[k], recv_sem=q_recv.at[k],
-            device_id={"seq": lax.rem(me + k, n)},
-        )
-        c.start()
-        q_copies.append(c)
+    step = 2 if n % 2 == 0 else 1
+    pair = me + 1 - 2 * lax.rem(me, 2)
+
+    def query_copy(c, slot, k, to):
+        return pltpu.make_async_remote_copy(
+            src_ref=gq.at[c, slot], dst_ref=gq.at[c, slot],
+            send_sem=q_send.at[c, k], recv_sem=q_recv.at[c, k], device_id={"seq": to},
+        )
+
+    far_first = sorted(range(1, n), key=lambda k: -min(k, n - k))
+    evens = [k for k in far_first if k % step == 0]
+    direct = [[] for _ in range(chunks)]
+    passed = [[] for _ in range(chunks)]
+    for c in range(chunks):
+        for k in evens:
+            cp = query_copy(c, me, k, lax.rem(me + k, n))
+            cp.start()
+            direct[c].append(cp)
+        if step == 2:
+            cp = query_copy(c, me, 1, pair)
+            cp.start()
+            passed[c].append(cp)
 
     row_head = lax.broadcasted_iota(jnp.int32, (H, groups), 0)
     row_head = (lax.div(row_head, hb) * hc + hr) * hb + lax.rem(row_head, hb)
@@ -86,23 +106,14 @@
         hit = jnp.where(tok < length, hit, 0.0)
         mask = jnp.dot(hot_b, hit.astype(bf16), preferred_element_type=f32)
         pen[r] = (1.0 - mask) * LOWEST
-    for r in range(R):
-        length = len_ref[r]
-        load_cache[r].wait()
-        x = cache[r].astype(f32)
-        live = tok_col < length
-        low = jnp.min(jnp.where(live, x, jnp.inf).reshape(pages, PAGE, D), axis=1)
-        high = jnp.max(jnp.where(live, x, -jnp.inf).reshape(pages, PAGE, D), axis=1)
-        live_page = page_col < length
-        lo_s[r] = jnp.where(live_page, low, 0.0).astype(bf16)
-        hi_s[r] = jnp.where(live_page, high, 0.0).astype(bf16)
-
-    for c in q_copies:
-        c.wait_recv()
-    for s in range(n):
-        block = gq[s].astype(f32)
-        for r in range(R):
-            qf[r, s * hb:(s + 1) * hb, :] = block[r * hb:(r + 1) * hb]
+    if step == 2:
+        for c in range(chunks):
+            for i in reversed(range(len(evens))):
+                k = evens[i]
+                direct[c][i].wait_recv()
+                cp = query_copy(c, lax.rem(me + n - k, n), k + 1, pair)
+                cp.start()
+                passed[c].append(cp)
 
     lane = lax.broadcasted_iota(jnp.int32, (H, 128), 1)
     tops = jnp.zeros((H, 128), f32)
@@ -110,13 +121,20 @@
     o_copies = []
     for c in range(chunks):
         outs = []
+        for cp in passed[c] if step == 2 else direct[c]:
+            cp.wait_recv()
+        for b in range(n):
+            block = gq[c, b].astype(f32)
+            for i in range(RC):
+                qf[c * RC + i, b * hb:(b + 1) * hb, :] = block[i * hb:(i + 1) * hb]
         for r in range(c * RC, (c + 1) * RC):
             q = qf[r].astype(bf16)
-            s = lax.dot_general(q, cache[r], NT, preferred_element_type=f32) * scale + pen[r]
+            load_cache[r].wait()
+            s = jnp.dot(q, cache[r], preferred_element_type=f32) * scale + pen[r]
             m = jnp.maximum(jnp.max(s, axis=1, keepdims=True), FLOOR)
             w = jnp.exp(s - m).astype(bf16)
             l = jnp.sum(w.astype(f32), axis=1, keepdims=True)
-            outs.append(jnp.dot(w, cache[r, :, :DL], preferred_element_type=f32))
+            outs.append(lax.dot_general(w, cache[r, :DL, :], NT, preferred_element_type=f32))
             tops = jnp.where(lane == r, m, tops)
             sums = jnp.where(lane == r, l, sums)
         for b in range(n):
@@ -127,7 +145,7 @@
             for b in range(n):
                 st[b, 0] = tops[b * hb:(b + 1) * hb]
                 st[b, 1] = sums[b * hb:(b + 1) * hb]
-        for k in range(1, n):
+        for k in far_first:
             to = lax.rem(me + k, n)
             cp = pltpu.make_async_remote_copy(
                 src_ref=so.at[c, to], dst_ref=ro.at[c, me],
@@ -143,6 +161,29 @@
                 cp.start()
                 o_copies.append(cp)
 
+    TILE = 128 if T % 128 == 0 else T
+    eye = jnp.where(
+        lax.broadcasted_iota(jnp.int32, (TILE, TILE), 0)
+        == lax.broadcasted_iota(jnp.int32, (TILE, TILE), 1), 1.0, 0.0
+    ).astype(bf16)
+    for r in range(R):
+        length = len_ref[r]
+        x = jnp.concatenate(
+            [
+                lax.dot_general(
+                    eye, cache[r, :, t * TILE:(t + 1) * TILE], NT, preferred_element_type=f32
+                )
+                for t in range(T // TILE)
+            ],
+            axis=0,
+        )
+        live = tok_col < length
+        low = jnp.min(jnp.where(live, x, jnp.inf).reshape(pages, PAGE, D), axis=1)
+        high = jnp.max(jnp.where(live, x, -jnp.inf).reshape(pages, PAGE, D), axis=1)
+        live_page = page_col < length
+        lo_s[r] = jnp.where(live_page, low, 0.0).astype(bf16)
+        hi_s[r] = jnp.where(live_page, high, 0.0).astype(bf16)
+
     parts = []
     for r in range(R):
         q = qf[r]
@@ -207,7 +248,7 @@
     res = jnp.dot(lhs, wuv[...].reshape(lhs.shape[1], wuv.shape[2]), preferred_element_type=f32)
     for r in range(R):
         out_ref[r] = res[r * hb:(r + 1) * hb].astype(bf16)
-    for cp in q_copies + o_copies + b_copies:
+    for cp in sum(direct + passed, []) + o_copies + b_copies:
         cp.wait_send()
 
 
@@ -223,21 +264,21 @@
     f32, bf16 = jnp.float32, jnp.bfloat16
     V = pltpu.VMEM
     vm = pl.BlockSpec(memory_space=pltpu.VMEM)
-    hbm = pl.BlockSpec(memory_space=pl.ANY)
+    hbm = pl.BlockSpec(memory_space=pltpu.HBM)
     dma = pltpu.SemaphoreType.DMA
     return pl.pallas_call(
         functools.partial(kernel, n, hc, R, hb, T, DL, D, groups, scale),
         out_shape=(
-            jax.ShapeDtypeStruct((R, hb, DV), bf16),
-            jax.ShapeDtypeStruct((R, groups, pages), f32),
+            V((R, hb, DV), bf16),
+            V((R, groups, pages), f32),
         ),
         in_specs=[pl.BlockSpec(memory_space=pltpu.SMEM), vm, vm, vm, hbm, hbm, hbm],
         out_specs=(vm, vm),
         scratch_shapes=[
             V((hb, DN, DL), bf16),
             V((hb, DL, DV), bf16),
-            V((R, T, D), bf16),
-            V((n, R * hb, D), bf16),
+            V((R, D, T), bf16),
+            V((chunks, n, R // chunks * hb, D), bf16),
             V((R, H, D), f32),
             V((R, H, T), f32),
             V((R, pages, D), bf16),
@@ -249,15 +290,16 @@
             V((groups, 128), f32),
             V((hc, groups, 128), f32),
             dma((2 + R,)),
-            dma((n,)), dma((n,)),
+            dma((hb,)),
+            dma((chunks, n)), dma((chunks, n)),
             dma((chunks, n)), dma((chunks, n)),
             dma((n,)), dma((n,)),
             dma((hc,)), dma((hc,)),
         ],
         compiler_params=pltpu.CompilerParams(
-            collective_id=0, has_side_effects=True, vmem_limit_bytes=40 * 1024 * 1024
+            collective_id=0, has_side_effects=True, vmem_limit_bytes=61000 * 1024
         ),
-    )(lengths, q_nope, q_rope, selected, w_uk, w_uv, cache)
+    )(lengths, q_nope, q_rope, selected, w_uk, w_uv, jnp.swapaxes(cache, 1, 2))
 
 
 def solution(mesh):

time: 31.6 us -> 25.8 us (0.82)
  local copies, waits for them, and re-layouts: 6.78 us -> 1.21 us
    unnamed x15 -> x2, local copies, waits for them, and re-layouts: 6.78 us -> 1.21 us
where the time goes in v3:
time: 25.8 us; the launch traced here: 25.6 us
  Pallas kernels  23.7 us (92%)
  local copies, waits for them, and re-layouts  1.21 us (5%)
  between operations  0.64 us (2%)
    pallas_call x1, Pallas kernels, local(): pl.pallas_call(functools.partial(kernel, n, hc, R, hb, T, DL, D, groups,...  23.7 us
    unnamed x2, local copies, waits for them, and re-layouts  1.21 us

profile of v3, /device:TPU:0, one launch (start us, length us, event | category | flops | bytes accessed | tf_op | source)
XLA Modules:
  0.0 25.6 jit_solution(11186492977290865917)
XLA Ops:
  0.6 23.7 %shard_map.86 = (bf16[4,8,128]{2,1,0:T(8,128)(2,1)S(1)}, f32[4,8,8]{2,1,0:T(8,128)S(1)}) custom-call(s32[4]{0:T(128)} %len_ref.1, bf16[4,8,128]{2,1,0:T(8,128)(2,1)} %qn_ref.1, bf16[4,8,64]{2,1,0:T(8,128)(2,1)} %qr_ref.1, s32[4,8,32]{2,1,0:T(8,128)} %sel_ref.1, bf16[8,128,512]{2,1,0:T(8,128)(2,1)} %wuk_hbm.1, bf16[8,512,128]{2,1,0:T(8,128)(2,1)} %wuv_hbm.1, ...), custom_call_target="tpu_custom_call" | custom-call | tf_op jit(solution)/shard_map/pallas_call | solution.py:269
  24.4 0.6 %copy.11 = bf16[4,8,128]{2,1,0:T(8,128)(2,1)} copy(bf16[4,8,128]{2,1,0:T(8,128)(2,1)S(1)} %get-tuple-element.2) | data formatting | bytes 16384
  25.0 0.6 %copy.12 = f32[4,8,8]{2,1,0:T(8,128)} copy(f32[4,8,8]{2,1,0:T(8,128)S(1)} %get-tuple-element.3) | data formatting | bytes 2048

commit v4 on v3

--- a/solution.py
+++ b/solution.py
@@ -116,8 +116,8 @@
                 passed[c].append(cp)
 
     lane = lax.broadcasted_iota(jnp.int32, (H, 128), 1)
-    tops = jnp.zeros((H, 128), f32)
-    sums = jnp.ones((H, 128), f32)
+    HALF = 64
+    stats = jnp.where(lane < HALF, 0.0, 1.0)
     o_copies = []
     for c in range(chunks):
         outs = []
@@ -135,16 +135,14 @@
             w = jnp.exp(s - m).astype(bf16)
             l = jnp.sum(w.astype(f32), axis=1, keepdims=True)
             outs.append(lax.dot_general(w, cache[r, :DL, :], NT, preferred_element_type=f32))
-            tops = jnp.where(lane == r, m, tops)
-            sums = jnp.where(lane == r, l, sums)
+            stats = jnp.where(lane == r, m, jnp.where(lane == HALF + r, l, stats))
         for b in range(n):
             so[c, b] = jnp.concatenate(
                 [o[b * hb:(b + 1) * hb] for o in outs], axis=0
             ).astype(bf16)
         if c == chunks - 1:
             for b in range(n):
-                st[b, 0] = tops[b * hb:(b + 1) * hb]
-                st[b, 1] = sums[b * hb:(b + 1) * hb]
+                st[b] = stats[b * hb:(b + 1) * hb]
         for k in far_first:
             to = lax.rem(me + k, n)
             cp = pltpu.make_async_remote_copy(
@@ -227,13 +225,13 @@
 
     for cp in o_copies:
         cp.wait_recv()
-    peak = rs[0, 0]
+    peak = rs[0]
     for b in range(1, n):
-        peak = jnp.maximum(peak, rs[b, 0])
-    shares = [jnp.exp(rs[b, 0] - peak) for b in range(n)]
-    total = shares[0] * rs[0, 1]
+        peak = jnp.maximum(peak, rs[b])
+    shares = [jnp.exp(rs[b] - peak) for b in range(n)]
+    total = shares[0] * pltpu.roll(rs[0], HALF, 1)
     for b in range(1, n):
-        total += shares[b] * rs[b, 1]
+        total += shares[b] * pltpu.roll(rs[b], HALF, 1)
     shares = [x / total for x in shares]
     rows = []
     for c in range(chunks):
@@ -259,7 +257,7 @@
     groups = selected.shape[1]
     pages = T // PAGE
     H = n * hb
-    chunks = 2 if R % 2 == 0 else 1
+    chunks = R
     scale = (DN + q_rope.shape[2]) ** (-0.5)
     f32, bf16 = jnp.float32, jnp.bfloat16
     V = pltpu.VMEM
@@ -284,9 +282,9 @@
             V((R, pages, D), bf16),
             V((R, pages, D), bf16),
             V((chunks, n, R // chunks * hb, DL), bf16),
-            V((n, 2, hb, 128), f32),
+            V((n, hb, 128), f32),
             V((chunks, n, R // chunks * hb, DL), bf16),
-            V((n, 2, hb, 128), f32),
+            V((n, hb, 128), f32),
             V((groups, 128), f32),
             V((hc, groups, 128), f32),
             dma((2 + R,)),

time: 25.8 us -> 25.1 us (0.973)
  Pallas kernels: 23.7 us -> 23 us
    pallas_call x1, Pallas kernels: 23.7 us -> 23 us  [local(): pl.pallas_call(functools.partial(kernel, n, hc, R, hb, T, DL, D, groups,...]
where the time goes in v4:
time: 25.1 us; the launch traced here: 24.8 us
  Pallas kernels  23 us (92%)
  local copies, waits for them, and re-layouts  1.21 us (5%)
  between operations  0.64 us (3%)
    pallas_call x1, Pallas kernels, local(): pl.pallas_call(functools.partial(kernel, n, hc, R, hb, T, DL, D, groups,...  23 us
    unnamed x2, local copies, waits for them, and re-layouts  1.21 us

profile of v4, /device:TPU:0, one launch (start us, length us, event | category | flops | bytes accessed | tf_op | source)
XLA Modules:
  0.0 24.8 jit_solution(8134052603513840832)
XLA Ops:
  0.6 23.0 %shard_map.86 = (bf16[4,8,128]{2,1,0:T(8,128)(2,1)S(1)}, f32[4,8,8]{2,1,0:T(8,128)S(1)}) custom-call(s32[4]{0:T(128)} %len_ref.1, bf16[4,8,128]{2,1,0:T(8,128)(2,1)} %qn_ref.1, bf16[4,8,64]{2,1,0:T(8,128)(2,1)} %qr_ref.1, s32[4,8,32]{2,1,0:T(8,128)} %sel_ref.1, bf16[8,128,512]{2,1,0:T(8,128)(2,1)} %wuk_hbm.1, bf16[8,512,128]{2,1,0:T(8,128)(2,1)} %wuv_hbm.1, ...), custom_call_target="tpu_custom_call" | custom-call | tf_op jit(solution)/shard_map/pallas_call | solution.py:267
  23.6 0.6 %copy.11 = bf16[4,8,128]{2,1,0:T(8,128)(2,1)} copy(bf16[4,8,128]{2,1,0:T(8,128)(2,1)S(1)} %get-tuple-element.2) | data formatting | bytes 16384
  24.2 0.6 %copy.12 = f32[4,8,8]{2,1,0:T(8,128)} copy(f32[4,8,8]{2,1,0:T(8,128)S(1)} %get-tuple-element.3) | data formatting | bytes 2048
